TPU v7x, 32 devices: a whole 2x2x4 slice. The times are simulated.
32 devices in a mesh: freq: 4 (over y, core), tcol: 8 (over z, x).
Axes of the slice: x: 2, y: 2, z: 4, core: 2. Of those that a mesh axis runs over, the one named last changes fastest.
Arguments:
- data: bfloat16 [4, 2, 4096, 128], P('freq', None, 'tcol'), may hold values from -6 to 6
- left_factor: bfloat16 [4, 2, 4096, 256], P('freq', None, 'tcol'), may hold values from -0.25 to 0.25
- right_factor: bfloat16 [4, 2, 4096, 256], P('freq', None, 'tcol'), may hold values from -0.1875 to 0.1875
- ranks: int32 [4, 8, 8], P('freq'), may hold values from 1 to 32
- freq_index: int32 [4], P('freq'), may hold values from 0 to 229
Outputs:
- wavefield: float32 [4, 2, 4096, 128], P('freq', None, 'tcol')
- residual: float32 [4, 2, 4096, 128], P('freq', None, 'tcol')
Inputs may be any that keep to these rules, and one draw needn't show every extreme that they name: `ranks`: the rank of each tile; factor columns at or beyond it are not part of the kernel.
All inputs are finite; a program needn't handle non-finite values.
Results may differ from a plain program's by a relative error of at most 0.006.
Values may be sent and summed in bfloat16 or wider, within the bound.
No kernel may reach another device: no remote copies, remote signals or barrier semaphores. Data moves between devices by JAX's collectives and lax.ppermute only.
A program may use at most 64 MiB of HBM per device.

v0:
```python
import jax
import jax.numpy as jnp
from jax import lax
from jax.sharding import PartitionSpec as P

ITERS = 3


def conj_left(factor, field):
    first = jnp.einsum(
        "ftq,fts->fqs", factor[:, 0], field[:, 0], preferred_element_type=jnp.float32
    )
    second = jnp.einsum(
        "ftq,fts->fqs", factor[:, 1], field[:, 1], preferred_element_type=jnp.float32
    )
    third = jnp.einsum(
        "ftq,fts->fqs", factor[:, 0], field[:, 1], preferred_element_type=jnp.float32
    )
    fourth = jnp.einsum(
        "ftq,fts->fqs", factor[:, 1], field[:, 0], preferred_element_type=jnp.float32
    )
    return jnp.stack([first + second, third - fourth], 1)


def plain_right(factor, coeffs):
    first = jnp.einsum(
        "ftq,fqs->fts", factor[:, 0], coeffs[:, 0], preferred_element_type=jnp.float32
    )
    second = jnp.einsum(
        "ftq,fqs->fts", factor[:, 1], coeffs[:, 1], preferred_element_type=jnp.float32
    )
    third = jnp.einsum(
        "ftq,fqs->fts", factor[:, 0], coeffs[:, 1], preferred_element_type=jnp.float32
    )
    fourth = jnp.einsum(
        "ftq,fqs->fts", factor[:, 1], coeffs[:, 0], preferred_element_type=jnp.float32
    )
    return jnp.stack([first - second, third + fourth], 1)


def body(data, left_factor, right_factor, ranks, freq_index):
    ntile = lax.axis_size("tcol")
    here = lax.axis_index("tcol")
    rank_width = left_factor.shape[3] // ntile
    levels = jnp.arange(rank_width)[None, None, :]
    column_ranks = lax.dynamic_slice_in_dim(ranks, here, 1, 2)[:, :, 0]
    row_ranks = lax.dynamic_slice_in_dim(ranks, here, 1, 1)[:, 0, :]
    colmask = (levels < column_ranks[:, :, None]).astype(jnp.float32).reshape(ranks.shape[0], -1)
    rowmask = (levels < row_ranks[:, :, None]).astype(jnp.float32).reshape(ranks.shape[0], -1)
    damping = (0.1 + 0.9 * freq_index.astype(jnp.float32) / 229.0)[:, None, None, None]
    residual = data.astype(jnp.float32)
    wavefield = jnp.zeros_like(residual)
    direction = jnp.zeros_like(residual)
    image = jnp.zeros_like(residual)
    for step in range(ITERS):
        coeffs = conj_left(left_factor, residual.astype(jnp.bfloat16))
        coeffs = (coeffs * rowmask[:, None, :, None]).astype(jnp.bfloat16)
        arrived = lax.all_to_all(coeffs, "tcol", split_axis=2, concat_axis=2, tiled=True)
        gradient = plain_right(right_factor, arrived) - damping * wavefield
        forward_coeffs = conj_left(right_factor, gradient.astype(jnp.bfloat16))
        forward_coeffs = (forward_coeffs * colmask[:, None, :, None]).astype(jnp.bfloat16)
        forward_arrived = lax.all_to_all(
            forward_coeffs, "tcol", split_axis=2, concat_axis=2, tiled=True
        )
        moved = plain_right(left_factor, forward_arrived)
        partial_sums = jnp.stack(
            [
                jnp.sum(moved * moved + damping * gradient * gradient, axis=(0, 1, 2)),
                jnp.sum(moved * image + damping * gradient * direction, axis=(0, 1, 2)),
                jnp.sum(image * image + damping * direction * direction, axis=(0, 1, 2)),
                jnp.sum(moved * residual - damping * gradient * wavefield, axis=(0, 1, 2)),
                jnp.sum(image * residual - damping * direction * wavefield, axis=(0, 1, 2)),
            ]
        )
        totals = lax.psum(partial_sums, ("freq", "tcol"))
        a11, a12, a22, b1, b2 = (totals[0], totals[1], totals[2], totals[3], totals[4])
        if step == 0:
            alpha = b1 / (1.1 * a11)
            beta = jnp.zeros_like(alpha)
        else:
            first = 1.1 * a11
            second = 1.1 * a22
            determinant = first * second - a12 * a12
            alpha = (b1 * second - a12 * b2) / determinant
            beta = (first * b2 - a12 * b1) / determinant
        direction = alpha * gradient + beta * direction
        image = alpha * moved + beta * image
        wavefield = wavefield + direction
        residual = residual - image
    return (wavefield, residual)


def solution(mesh):
    in_specs = (
        P("freq", None, "tcol", None),
        P("freq", None, "tcol", None),
        P("freq", None, "tcol", None),
        P("freq", None, None),
        P("freq"),
    )
    out_specs = (P("freq", None, "tcol", None), P("freq", None, "tcol", None))
    return jax.shard_map(body, mesh=mesh, in_specs=in_specs, out_specs=out_specs, check_vma=False)
```

profile of v0, /device:TPU:0, one launch (start us, length us, event | category | flops | bytes accessed | tf_op | source)
XLA Modules:
  0.0 213.9 jit_solution(10456277240478988102)
XLA Ops:
  0.7 0.7 copy-done
  1.5 1.2 fusion.116
  2.8 1.2 fusion.118
  5.1 0.8 copy.35
  5.9 7.3 %all-to-all-start = ((bf16[1,2,256,128]{3,1,0,2:T(2,128)(2,1)}), bf16[1,2,256,128]{3,1,0,2:T(2,128)(2,1)S(1)}, u32[]{:S(2)}, u32[]{:S(2)}) async-start(bf16[1,2,256,128]{3,1,0,2:T(2,128)(2,1)} %copy.35), calls=%async_computation | async-start | bytes 262144 | tf_op jit(solution)/shard_map/all_to_all | solution.py:58
  13.8 6.7 %all-to-all-done = bf16[1,2,256,128]{3,1,0,2:T(2,128)(2,1)S(1)} async-done(((bf16[1,2,256,128]{3,1,0,2:T(2,128)(2,1)}), bf16[1,2,256,128]{3,1,0,2:T(2,128)(2,1)S(1)}, u32[]{:S(2)}, u32[]{:S(2)}) %all-to-all-start) | async-done | bytes 131104 | tf_op jit(solution)/shard_map/all_to_all | solution.py:58
  22.5 0.8 copy.38
  23.3 3.4 %all-to-all-start.1 = ((bf16[1,2,256,128]{3,1,0,2:T(2,128)(2,1)}), bf16[1,2,256,128]{3,1,0,2:T(2,128)(2,1)S(1)}, u32[]{:S(2)}, u32[]{:S(2)}) async-start(bf16[1,2,256,128]{3,1,0,2:T(2,128)(2,1)} %copy.38), calls=%async_computation.1 | async-start | bytes 262144 | tf_op jit(solution)/shard_map/all_to_all | solution.py:62
  26.8 7.1 %all-to-all-done.1 = bf16[1,2,256,128]{3,1,0,2:T(2,128)(2,1)S(1)} async-done(((bf16[1,2,256,128]{3,1,0,2:T(2,128)(2,1)}), bf16[1,2,256,128]{3,1,0,2:T(2,128)(2,1)S(1)}, u32[]{:S(2)}, u32[]{:S(2)}) %all-to-all-start.1) | async-done | bytes 131104 | tf_op jit(solution)/shard_map/all_to_all | solution.py:62
  35.5 38.5 %psum.21 = f32[5,128]{1,0:T(8,128)S(1)} all-reduce(f32[5,128]{1,0:T(8,128)S(1)} %stack.179), channel_id=1, replica_groups=mesh['freq'=4,'tcol'=8] {'freq','tcol'}, use_global_device_ids=true, to_apply=%region_4.0 | all-reduce | flops 640 | bytes 5120 | tf_op jit(solution)/shard_map/psum | solution.py:75
  75.5 11.7 %all_to_all.30 = bf16[1,2,256,128]{3,1,0,2:T(2,128)(2,1)S(1)} all-to-all(bf16[1,2,256,128]{3,1,0,2:T(2,128)(2,1)S(1)} %copy.46), channel_id=1, replica_groups=mesh['freq'=4,'tcol'=8] {'tcol'}, dimensions={2} | all-to-all | bytes 262144 | tf_op jit(solution)/shard_map/all_to_all | solution.py:58
  89.5 9.7 %all_to_all.31 = bf16[1,2,256,128]{3,1,0,2:T(2,128)(2,1)S(1)} all-to-all(bf16[1,2,256,128]{3,1,0,2:T(2,128)(2,1)S(1)} %copy.49), channel_id=1, replica_groups=mesh['freq'=4,'tcol'=8] {'tcol'}, dimensions={2} | all-to-all | bytes 262144 | tf_op jit(solution)/shard_map/all_to_all | solution.py:62
  101.0 0.6 subtract_reduce_fusion
  101.7 38.3 %psum.22 = f32[5,128]{1,0:T(8,128)S(1)} all-reduce(f32[5,128]{1,0:T(8,128)S(1)} %stack.197), channel_id=1, replica_groups=mesh['freq'=4,'tcol'=8] {'freq','tcol'}, use_global_device_ids=true, to_apply=%region_10.0 | all-reduce | flops 640 | bytes 5120 | tf_op jit(solution)/shard_map/psum | solution.py:75
  139.9 2.1 fusion.186
  143.3 11.7 %all_to_all.32 = bf16[1,2,256,128]{3,1,0,2:T(2,128)(2,1)S(1)} all-to-all(bf16[1,2,256,128]{3,1,0,2:T(2,128)(2,1)S(1)} %copy.56), channel_id=1, replica_groups=mesh['freq'=4,'tcol'=8] {'tcol'}, dimensions={2} | all-to-all | bytes 262144 | tf_op jit(solution)/shard_map/all_to_all | solution.py:58
  156.2 1.1 fusion.185
  158.2 9.7 %all_to_all.33 = bf16[1,2,256,128]{3,1,0,2:T(2,128)(2,1)S(1)} all-to-all(bf16[1,2,256,128]{3,1,0,2:T(2,128)(2,1)S(1)} %copy.59), channel_id=1, replica_groups=mesh['freq'=4,'tcol'=8] {'tcol'}, dimensions={2} | all-to-all | bytes 262144 | tf_op jit(solution)/shard_map/all_to_all | solution.py:62
  169.1 0.5 copy-done.4
  169.9 0.7 fusion.37
  170.7 38.3 %psum.23 = f32[5,128]{1,0:T(8,128)S(1)} all-reduce(f32[5,128]{1,0:T(8,128)S(1)} %stack.215), channel_id=1, replica_groups=mesh['freq'=4,'tcol'=8] {'freq','tcol'}, use_global_device_ids=true, to_apply=%region_16.0 | all-reduce | flops 640 | bytes 5120 | tf_op jit(solution)/shard_map/psum | solution.py:75
  209.0 2.0 add_subtract_fusion
  210.9 2.0 copy.63
  213.0 1.0 copy.62
  (99 shorter events, 15.0 us)
Async XLA Ops:
  0.6 0.7 copy-start
  0.6 2.1 copy-start.2
  2.8 1.6 copy-start.8
  5.1 15.6 %copy-start.1 = (bf16[1,2,512,256]{3,2,1,0:T(8,128)(2,1)S(1)}, bf16[1,2,512,256]{3,2,1,0:T(8,128)(2,1)}, u32[]{:S(2)}) copy-start(bf16[1,2,512,256]{3,2,1,0:T(8,128)(2,1)} %param.7) | copy-start | bytes 1572868
  5.9 14.6 %all-to-all-start = ((bf16[1,2,256,128]{3,1,0,2:T(2,128)(2,1)}), bf16[1,2,256,128]{3,1,0,2:T(2,128)(2,1)S(1)}, u32[]{:S(2)}, u32[]{:S(2)}) async-start(bf16[1,2,256,128]{3,1,0,2:T(2,128)(2,1)} %copy.35), calls=%async_computation | async-start | bytes 262144 | tf_op jit(solution)/shard_map/all_to_all | solution.py:58
  23.3 10.7 %all-to-all-start.1 = ((bf16[1,2,256,128]{3,1,0,2:T(2,128)(2,1)}), bf16[1,2,256,128]{3,1,0,2:T(2,128)(2,1)S(1)}, u32[]{:S(2)}, u32[]{:S(2)}) async-start(bf16[1,2,256,128]{3,1,0,2:T(2,128)(2,1)} %copy.38), calls=%async_computation.1 | async-start | bytes 262144 | tf_op jit(solution)/shard_map/all_to_all | solution.py:62
  100.1 0.7 copy-start.5
  100.3 0.7 copy-start.6
  168.6 1.0 copy-start.4
  168.9 1.1 copy-start.3
  169.1 1.5 copy-start.7
where the time goes:
time: 215 us; the launch traced here: 214 us
  blocking collectives  158 us (73%)
  waiting for transfers between devices  13.8 us (6%)
  matrix products  13 us (6%)
  starting transfers between devices  10.7 us (5%)
  local copies, waits for them, and re-layouts  8.86 us (4%)
  other arithmetic  7.88 us (4%)
    psum x3, blocking collectives, body(): totals = lax.psum(partial_sums, ('freq', 'tcol'))  115 us
    all_to_all x2, blocking collectives, body(): lax.all_to_all(coeffs, 'tcol', split_axis=2, concat_axis=2, tiled=True)  23.4 us
    all_to_all x2, blocking collectives, body(): lax.all_to_all(forward_coeffs, 'tcol', split_axis=2, concat_axis=2, tiled...  19.5 us
    all_to_all x1, starting transfers between devices, body(): lax.all_to_all(coeffs, 'tcol', split_axis=2, concat_axis=2, tiled=True)  7.28 us
    all_to_all x1, waiting for transfers between devices, body(): lax.all_to_all(forward_coeffs, 'tcol', split_axis=2, concat_axis=2, tiled...  7.12 us
    all_to_all x1, waiting for transfers between devices, body(): lax.all_to_all(coeffs, 'tcol', split_axis=2, concat_axis=2, tiled=True)  6.69 us
    unnamed x21, local copies, waits for them, and re-layouts  5.08 us
  transfers between devices with their start and end apart: 2, of which 2 were waited for; matrix products, arithmetic and copies ran while one was open for 0% of the time, Pallas kernels for 0%

commit v1 on v0

--- a/solution.py
+++ b/solution.py
@@ -59,9 +59,20 @@
         gradient = plain_right(right_factor, arrived) - damping * wavefield
         forward_coeffs = conj_left(right_factor, gradient.astype(jnp.bfloat16))
         forward_coeffs = (forward_coeffs * colmask[:, None, :, None]).astype(jnp.bfloat16)
-        forward_arrived = lax.all_to_all(
-            forward_coeffs, "tcol", split_axis=2, concat_axis=2, tiled=True
-        )
+        ways, here_2 = (lax.axis_size("tcol"), lax.axis_index("tcol"))
+        width = forward_coeffs.shape[2] // ways
+        dims = list(forward_coeffs.shape)
+        dims[2] = width
+        height = dims[2]
+        dims[2] = height * ways
+        forward_arrived = jnp.zeros(dims, forward_coeffs.dtype)
+        for mask in range(ways):
+            part = lax.dynamic_slice_in_dim(forward_coeffs, (here_2 ^ mask) * width, width, axis=2)
+            if mask:
+                part = lax.ppermute(part, "tcol", [(d, d ^ mask) for d in range(ways)])
+            forward_arrived = lax.dynamic_update_slice_in_dim(
+                forward_arrived, part, (here_2 ^ mask) * height, axis=2
+            )
         moved = plain_right(left_factor, forward_arrived)
         partial_sums = jnp.stack(
             [

time: 215 us -> 236 us (1.098)
  starting transfers between devices: 10.7 us -> 40.9 us
  blocking collectives: 158 us -> 138 us
  local copies, waits for them, and re-layouts: 8.86 us -> 26.1 us
  waiting for transfers between devices: 13.8 us -> 6.72 us
    ppermute x0 -> x21, starting transfers between devices: none -> 33.6 us  [body(): part = lax.ppermute(part, 'tcol', [(d, d ^ mask) for d in range(ways)])]
    all_to_all x2 -> x0, blocking collectives: 19.5 us -> none  [body(): lax.all_to_all(forward_coeffs, 'tcol', split_axis=2, concat_axis=2, tiled...]
    dynamic_update_slice x0 -> x24, local copies, waits for them, and re-layouts: none -> 17.4 us  [body(): lax.dynamic_update_slice_in_dim(forward_arrived, part, (here_2 ^ mask) *...]
    all_to_all x1 -> x0, waiting for transfers between devices: 7.12 us -> none  [body(): lax.all_to_all(forward_coeffs, 'tcol', split_axis=2, concat_axis=2, tiled...]
    all_to_all x1 -> x0, starting transfers between devices: 3.37 us -> none  [body(): lax.all_to_all(forward_coeffs, 'tcol', split_axis=2, concat_axis=2, tiled...]
    unnamed x21 -> x27, local copies, waits for them, and re-layouts: 5.08 us -> 5.71 us
  transfers between devices with their start and end apart: 2 -> 22, of which waited for: 2 -> 1; matrix products, arithmetic and copies ran while one was open for 0% -> 6% of each run, Pallas kernels for 0% -> 0%
where the time goes in v1:
time: 236 us; the launch traced here: 235 us
  blocking collectives  138 us (58%)
  starting transfers between devices  40.9 us (17%)
  local copies, waits for them, and re-layouts  26.1 us (11%)
  matrix products  12.9 us (5%)
  other arithmetic  7.89 us (3%)
  waiting for transfers between devices  6.72 us (3%)
    psum x3, blocking collectives, body(): totals = lax.psum(partial_sums, ('freq', 'tcol'))  113 us
    ppermute x21, starting transfers between devices, body(): part = lax.ppermute(part, 'tcol', [(d, d ^ mask) for d in range(ways)])  33.6 us
    all_to_all x2, blocking collectives, body(): lax.all_to_all(coeffs, 'tcol', split_axis=2, concat_axis=2, tiled=True)  25.5 us
    dynamic_update_slice x24, local copies, waits for them, and re-layouts, body(): lax.dynamic_update_slice_in_dim(forward_arrived, part, (here_2 ^ mask) *...  17.4 us
    all_to_all x1, starting transfers between devices, body(): lax.all_to_all(coeffs, 'tcol', split_axis=2, concat_axis=2, tiled=True)  7.28 us
    all_to_all x1, waiting for transfers between devices, body(): lax.all_to_all(coeffs, 'tcol', split_axis=2, concat_axis=2, tiled=True)  6.67 us
    unnamed x27, local copies, waits for them, and re-layouts  5.71 us
  transfers between devices with their start and end apart: 22, of which 1 were waited for; matrix products, arithmetic and copies ran while one was open for 6% of the time, Pallas kernels for 0%

profile of v1, /device:TPU:0, one launch (start us, length us, event | category | flops | bytes accessed | tf_op | source)
XLA Modules:
  0.0 235.0 jit_solution(5324757415346695663)
XLA Ops:
  5.9 7.3 %all-to-all-start = ((bf16[1,2,256,128]{3,1,0,2:T(2,128)(2,1)}), bf16[1,2,256,128]{3,1,0,2:T(2,128)(2,1)S(1)}, u32[]{:S(2)}, u32[]{:S(2)}) async-start(bf16[1,2,256,128]{3,1,0,2:T(2,128)(2,1)} %copy.32), calls=%async_computation | async-start | bytes 262144 | tf_op jit(solution)/shard_map/all_to_all | solution.py:58
  13.8 6.7 %all-to-all-done = bf16[1,2,256,128]{3,1,0,2:T(2,128)(2,1)S(1)} async-done(((bf16[1,2,256,128]{3,1,0,2:T(2,128)(2,1)}), bf16[1,2,256,128]{3,1,0,2:T(2,128)(2,1)S(1)}, u32[]{:S(2)}, u32[]{:S(2)}) %all-to-all-start) | async-done | bytes 131104 | tf_op jit(solution)/shard_map/all_to_all | solution.py:58
  22.8 1.3 collective-permute-start
  26.3 2.5 %collective-permute-start.3 = (bf16[1,2,32,128]{2,3,1,0:T(8,128)(2,1)S(1)}, bf16[1,2,32,128]{2,3,1,0:T(8,128)(2,1)S(1)}, u32[]{:S(2)}, u32[]{:S(2)}) collective-permute-start(bf16[1,2,32,128]{2,3,1,0:T(8,128)(2,1)S(1)} %get-tuple-element.52), channel_id=1, source_target_pairs={{0,4},{1,5},{2,6},{3,7},{4,0},{5,1},{6,2},{7,3},{8,12},{9,13},{10,... | collective-permute-start | bytes 49160 | tf_op jit(solution)/shard_map/ppermute | solution.py:72
  28.9 1.4 collective-permute-start.5
  30.3 3.6 %collective-permute-start.6 = (bf16[1,2,32,128]{2,3,1,0:T(8,128)(2,1)S(1)}, bf16[1,2,32,128]{2,3,1,0:T(8,128)(2,1)S(1)}, u32[]{:S(2)}, u32[]{:S(2)}) collective-permute-start(bf16[1,2,32,128]{2,3,1,0:T(8,128)(2,1)S(1)} %get-tuple-element.49), channel_id=1, source_target_pairs={{0,7},{1,6},{2,5},{3,4},{4,3},{5,2},{6,1},{7,0},{8,15},{9,14},{10,... | collective-permute-start | bytes 49160 | tf_op jit(solution)/shard_map/ppermute | solution.py:72
  40.4 39.0 %psum.21 = f32[5,128]{1,0:T(8,128)S(1)} all-reduce(f32[5,128]{1,0:T(8,128)S(1)} %stack.179), channel_id=1, replica_groups=mesh['freq'=4,'tcol'=8] {'freq','tcol'}, use_global_device_ids=true, to_apply=%region_4.0 | all-reduce | flops 640 | bytes 5120 | tf_op jit(solution)/shard_map/psum | solution.py:86
  80.9 12.4 %all_to_all.15 = bf16[1,2,256,128]{3,1,0,2:T(2,128)(2,1)S(1)} all-to-all(bf16[1,2,256,128]{3,1,0,2:T(2,128)(2,1)S(1)} %copy.40), channel_id=1, replica_groups=mesh['freq'=4,'tcol'=8] {'tcol'}, dimensions={2} | all-to-all | bytes 262144 | tf_op jit(solution)/shard_map/all_to_all | solution.py:58
  95.7 1.3 collective-permute-start.7
  99.2 2.5 %collective-permute-start.10 = (bf16[1,2,32,128]{2,3,1,0:T(8,128)(2,1)S(1)}, bf16[1,2,32,128]{2,3,1,0:T(8,128)(2,1)}, u32[]{:S(2)}, u32[]{:S(2)}) collective-permute-start(bf16[1,2,32,128]{2,3,1,0:T(8,128)(2,1)S(1)} %get-tuple-element.42), channel_id=1, source_target_pairs={{0,4},{1,5},{2,6},{3,7},{4,0},{5,1},{6,2},{7,3},{8,12},{9,13},{10,... | collective-permute-start | bytes 49160 | tf_op jit(solution)/shard_map/ppermute | solution.py:72
  102.4 1.4 collective-permute-start.12
  103.8 3.6 %collective-permute-start.13 = (bf16[1,2,32,128]{2,3,1,0:T(8,128)(2,1)S(1)}, bf16[1,2,32,128]{2,3,1,0:T(8,128)(2,1)}, u32[]{:S(2)}, u32[]{:S(2)}) collective-permute-start(bf16[1,2,32,128]{2,3,1,0:T(8,128)(2,1)S(1)} %get-tuple-element.39), channel_id=1, source_target_pairs={{0,7},{1,6},{2,5},{3,4},{4,3},{5,2},{6,1},{7,0},{8,15},{9,14},{10,... | collective-permute-start | bytes 49160 | tf_op jit(solution)/shard_map/ppermute | solution.py:72
  107.8 1.5 dynamic_update_slice.81
  110.1 1.5 dynamic_update_slice.83
  114.0 1.4 dynamic_update_slice.87
  117.7 36.9 %psum.22 = f32[5,128]{1,0:T(8,128)S(1)} all-reduce(f32[5,128]{1,0:T(8,128)S(1)} %stack.197), channel_id=1, replica_groups=mesh['freq'=4,'tcol'=8] {'freq','tcol'}, use_global_device_ids=true, to_apply=%region_10.0 | all-reduce | flops 640 | bytes 5120 | tf_op jit(solution)/shard_map/psum | solution.py:86
  154.5 2.1 fusion.188
  158.0 13.1 %all_to_all.16 = bf16[1,2,256,128]{3,1,0,2:T(2,128)(2,1)S(1)} all-to-all(bf16[1,2,256,128]{3,1,0,2:T(2,128)(2,1)S(1)} %copy.47), channel_id=1, replica_groups=mesh['freq'=4,'tcol'=8] {'tcol'}, dimensions={2} | all-to-all | bytes 262144 | tf_op jit(solution)/shard_map/all_to_all | solution.py:58
  177.9 2.5 %collective-permute-start.17 = (bf16[1,2,32,128]{2,3,1,0:T(8,128)(2,1)S(1)}, bf16[1,2,32,128]{2,3,1,0:T(8,128)(2,1)S(1)}, u32[]{:S(2)}, u32[]{:S(2)}) collective-permute-start(bf16[1,2,32,128]{2,3,1,0:T(8,128)(2,1)S(1)} %get-tuple-element.32), channel_id=1, source_target_pairs={{0,4},{1,5},{2,6},{3,7},{4,0},{5,1},{6,2},{7,3},{8,12},{9,13},{10,... | collective-permute-start | bytes 49160 | tf_op jit(solution)/shard_map/ppermute | solution.py:72
  180.5 1.4 collective-permute-start.19
  181.9 3.6 %collective-permute-start.20 = (bf16[1,2,32,128]{2,3,1,0:T(8,128)(2,1)S(1)}, bf16[1,2,32,128]{2,3,1,0:T(8,128)(2,1)S(1)}, u32[]{:S(2)}, u32[]{:S(2)}) collective-permute-start(bf16[1,2,32,128]{2,3,1,0:T(8,128)(2,1)S(1)} %get-tuple-element.29), channel_id=1, source_target_pairs={{0,7},{1,6},{2,5},{3,4},{4,3},{5,2},{6,1},{7,0},{8,15},{9,14},{10,... | collective-permute-start | bytes 49160 | tf_op jit(solution)/shard_map/ppermute | solution.py:72
  193.0 37.0 %psum.23 = f32[5,128]{1,0:T(8,128)S(1)} all-reduce(f32[5,128]{1,0:T(8,128)S(1)} %stack.215), channel_id=1, replica_groups=mesh['freq'=4,'tcol'=8] {'freq','tcol'}, use_global_device_ids=true, to_apply=%region_16.0 | all-reduce | flops 640 | bytes 5120 | tf_op jit(solution)/shard_map/psum | solution.py:86
  230.0 2.0 add_subtract_fusion
  231.9 2.0 copy.51
  (167 shorter events, 44.6 us)
Async XLA Ops:
  5.1 15.6 %copy-start.1 = (bf16[1,2,512,256]{3,2,1,0:T(8,128)(2,1)S(1)}, bf16[1,2,512,256]{3,2,1,0:T(8,128)(2,1)}, u32[]{:S(2)}) copy-start(bf16[1,2,512,256]{3,2,1,0:T(8,128)(2,1)} %param.7) | copy-start | bytes 1572868
  5.9 14.6 %all-to-all-start = ((bf16[1,2,256,128]{3,1,0,2:T(2,128)(2,1)}), bf16[1,2,256,128]{3,1,0,2:T(2,128)(2,1)S(1)}, u32[]{:S(2)}, u32[]{:S(2)}) async-start(bf16[1,2,256,128]{3,1,0,2:T(2,128)(2,1)} %copy.32), calls=%async_computation | async-start | bytes 262144 | tf_op jit(solution)/shard_map/all_to_all | solution.py:58
  22.7 6.1 %collective-permute-start.1 = (bf16[1,2,32,128]{2,3,1,0:T(8,128)(2,1)S(1)}, bf16[1,2,32,128]{2,3,1,0:T(8,128)(2,1)S(1)}, u32[]{:S(2)}, u32[]{:S(2)}) collective-permute-start(bf16[1,2,32,128]{2,3,1,0:T(8,128)(2,1)S(1)} %get-tuple-element.54), channel_id=1, source_target_pairs={{0,2},{1,3},{2,0},{3,1},{4,6},{5,7},{6,4},{7,5},{8,10},{9,11},{10,... | collective-permute-start | bytes 49160 | tf_op jit(solution)/shard_map/ppermute | solution.py:72
  22.8 7.5 %collective-permute-start = (bf16[1,2,32,128]{2,3,1,0:T(8,128)(2,1)S(1)}, bf16[1,2,32,128]{2,3,1,0:T(8,128)(2,1)S(1)}, u32[]{:S(2)}, u32[]{:S(2)}) collective-permute-start(bf16[1,2,32,128]{2,3,1,0:T(8,128)(2,1)S(1)} %get-tuple-element.55), channel_id=1, source_target_pairs={{0,1},{1,0},{2,3},{3,2},{4,5},{5,4},{6,7},{7,6},{8,9},{9,8},{10,11... | collective-permute-start | bytes 49160 | tf_op jit(solution)/shard_map/ppermute | solution.py:72
  24.1 12.8 %collective-permute-start.4 = (bf16[1,2,32,128]{2,3,1,0:T(8,128)(2,1)S(1)}, bf16[1,2,32,128]{2,3,1,0:T(8,128)(2,1)S(1)}, u32[]{:S(2)}, u32[]{:S(2)}) collective-permute-start(bf16[1,2,32,128]{2,3,1,0:T(8,128)(2,1)S(1)} %get-tuple-element.51), channel_id=1, source_target_pairs={{0,5},{1,4},{2,7},{3,6},{4,1},{5,0},{6,3},{7,2},{8,13},{9,12},{10,... | collective-permute-start | bytes 49160 | tf_op jit(solution)/shard_map/ppermute | solution.py:72
  25.4 10.5 %collective-permute-start.2 = (bf16[1,2,32,128]{2,3,1,0:T(8,128)(2,1)S(1)}, bf16[1,2,32,128]{2,3,1,0:T(8,128)(2,1)S(1)}, u32[]{:S(2)}, u32[]{:S(2)}) collective-permute-start(bf16[1,2,32,128]{2,3,1,0:T(8,128)(2,1)S(1)} %get-tuple-element.53), channel_id=1, source_target_pairs={{0,3},{1,2},{2,1},{3,0},{4,7},{5,6},{6,5},{7,4},{8,11},{9,10},{10,... | collective-permute-start | bytes 49160 | tf_op jit(solution)/shard_map/ppermute | solution.py:72
  26.3 10.3 %collective-permute-start.3 = (bf16[1,2,32,128]{2,3,1,0:T(8,128)(2,1)S(1)}, bf16[1,2,32,128]{2,3,1,0:T(8,128)(2,1)S(1)}, u32[]{:S(2)}, u32[]{:S(2)}) collective-permute-start(bf16[1,2,32,128]{2,3,1,0:T(8,128)(2,1)S(1)} %get-tuple-element.52), channel_id=1, source_target_pairs={{0,4},{1,5},{2,6},{3,7},{4,0},{5,1},{6,2},{7,3},{8,12},{9,13},{10,... | collective-permute-start | bytes 49160 | tf_op jit(solution)/shard_map/ppermute | solution.py:72
  28.9 8.8 %collective-permute-start.5 = (bf16[1,2,32,128]{2,3,1,0:T(8,128)(2,1)S(1)}, bf16[1,2,32,128]{2,3,1,0:T(8,128)(2,1)S(1)}, u32[]{:S(2)}, u32[]{:S(2)}) collective-permute-start(bf16[1,2,32,128]{2,3,1,0:T(8,128)(2,1)S(1)} %get-tuple-element.50), channel_id=1, source_target_pairs={{0,6},{1,7},{2,4},{3,5},{4,2},{5,3},{6,0},{7,1},{8,14},{9,15},{10,... | collective-permute-start | bytes 49160 | tf_op jit(solution)/shard_map/ppermute | solution.py:72
  30.3 8.0 %collective-permute-start.6 = (bf16[1,2,32,128]{2,3,1,0:T(8,128)(2,1)S(1)}, bf16[1,2,32,128]{2,3,1,0:T(8,128)(2,1)S(1)}, u32[]{:S(2)}, u32[]{:S(2)}) collective-permute-start(bf16[1,2,32,128]{2,3,1,0:T(8,128)(2,1)S(1)} %get-tuple-element.49), channel_id=1, source_target_pairs={{0,7},{1,6},{2,5},{3,4},{4,3},{5,2},{6,1},{7,0},{8,15},{9,14},{10,... | collective-permute-start | bytes 49160 | tf_op jit(solution)/shard_map/ppermute | solution.py:72
  95.6 6.1 %collective-permute-start.8 = (bf16[1,2,32,128]{2,3,1,0:T(8,128)(2,1)S(1)}, bf16[1,2,32,128]{2,3,1,0:T(8,128)(2,1)S(1)}, u32[]{:S(2)}, u32[]{:S(2)}) collective-permute-start(bf16[1,2,32,128]{2,3,1,0:T(8,128)(2,1)S(1)} %get-tuple-element.44), channel_id=1, source_target_pairs={{0,2},{1,3},{2,0},{3,1},{4,6},{5,7},{6,4},{7,5},{8,10},{9,11},{10,... | collective-permute-start | bytes 49160 | tf_op jit(solution)/shard_map/ppermute | solution.py:72
  95.7 8.1 %collective-permute-start.7 = (bf16[1,2,32,128]{2,3,1,0:T(8,128)(2,1)S(1)}, bf16[1,2,32,128]{2,3,1,0:T(8,128)(2,1)S(1)}, u32[]{:S(2)}, u32[]{:S(2)}) collective-permute-start(bf16[1,2,32,128]{2,3,1,0:T(8,128)(2,1)S(1)} %get-tuple-element.45), channel_id=1, source_target_pairs={{0,1},{1,0},{2,3},{3,2},{4,5},{5,4},{6,7},{7,6},{8,9},{9,8},{10,11... | collective-permute-start | bytes 49160 | tf_op jit(solution)/shard_map/ppermute | solution.py:72
  97.0 15.6 %collective-permute-start.11 = (bf16[1,2,32,128]{2,3,1,0:T(8,128)(2,1)S(1)}, bf16[1,2,32,128]{2,3,1,0:T(8,128)(2,1)S(1)}, u32[]{:S(2)}, u32[]{:S(2)}) collective-permute-start(bf16[1,2,32,128]{2,3,1,0:T(8,128)(2,1)S(1)} %get-tuple-element.41), channel_id=1, source_target_pairs={{0,5},{1,4},{2,7},{3,6},{4,1},{5,0},{6,3},{7,2},{8,13},{9,12},{10,... | collective-permute-start | bytes 49160 | tf_op jit(solution)/shard_map/ppermute | solution.py:72
  98.3 11.8 %collective-permute-start.9 = (bf16[1,2,32,128]{2,3,1,0:T(8,128)(2,1)S(1)}, bf16[1,2,32,128]{2,3,1,0:T(8,128)(2,1)}, u32[]{:S(2)}, u32[]{:S(2)}) collective-permute-start(bf16[1,2,32,128]{2,3,1,0:T(8,128)(2,1)S(1)} %get-tuple-element.43), channel_id=1, source_target_pairs={{0,3},{1,2},{2,1},{3,0},{4,7},{5,6},{6,5},{7,4},{8,11},{9,10},{10,... | collective-permute-start | bytes 49160 | tf_op jit(solution)/shard_map/ppermute | solution.py:72
  99.2 12.3 %collective-permute-start.10 = (bf16[1,2,32,128]{2,3,1,0:T(8,128)(2,1)S(1)}, bf16[1,2,32,128]{2,3,1,0:T(8,128)(2,1)}, u32[]{:S(2)}, u32[]{:S(2)}) collective-permute-start(bf16[1,2,32,128]{2,3,1,0:T(8,128)(2,1)S(1)} %get-tuple-element.42), channel_id=1, source_target_pairs={{0,4},{1,5},{2,6},{3,7},{4,0},{5,1},{6,2},{7,3},{8,12},{9,13},{10,... | collective-permute-start | bytes 49160 | tf_op jit(solution)/shard_map/ppermute | solution.py:72
  102.4 10.9 %collective-permute-start.12 = (bf16[1,2,32,128]{2,3,1,0:T(8,128)(2,1)S(1)}, bf16[1,2,32,128]{2,3,1,0:T(8,128)(2,1)S(1)}, u32[]{:S(2)}, u32[]{:S(2)}) collective-permute-start(bf16[1,2,32,128]{2,3,1,0:T(8,128)(2,1)S(1)} %get-tuple-element.40), channel_id=1, source_target_pairs={{0,6},{1,7},{2,4},{3,5},{4,2},{5,3},{6,0},{7,1},{8,14},{9,15},{10,... | collective-permute-start | bytes 49160 | tf_op jit(solution)/shard_map/ppermute | solution.py:72
  103.8 3.6 %copy-start.11 = (bf16[1,2,32,128]{2,3,1,0:T(8,128)(2,1)}, bf16[1,2,32,128]{2,3,1,0:T(8,128)(2,1)S(1)}, u32[]{:S(2)}) copy-start(bf16[1,2,32,128]{2,3,1,0:T(8,128)(2,1)S(1)} %collective-permute-done.7) | copy-start | bytes 49156
  103.8 10.1 %collective-permute-start.13 = (bf16[1,2,32,128]{2,3,1,0:T(8,128)(2,1)S(1)}, bf16[1,2,32,128]{2,3,1,0:T(8,128)(2,1)}, u32[]{:S(2)}, u32[]{:S(2)}) collective-permute-start(bf16[1,2,32,128]{2,3,1,0:T(8,128)(2,1)S(1)} %get-tuple-element.39), channel_id=1, source_target_pairs={{0,7},{1,6},{2,5},{3,4},{4,3},{5,2},{6,1},{7,0},{8,15},{9,14},{10,... | collective-permute-start | bytes 49160 | tf_op jit(solution)/shard_map/ppermute | solution.py:72
  174.4 6.1 %collective-permute-start.15 = (bf16[1,2,32,128]{2,3,1,0:T(8,128)(2,1)S(1)}, bf16[1,2,32,128]{2,3,1,0:T(8,128)(2,1)S(1)}, u32[]{:S(2)}, u32[]{:S(2)}) collective-permute-start(bf16[1,2,32,128]{2,3,1,0:T(8,128)(2,1)S(1)} %get-tuple-element.34), channel_id=1, source_target_pairs={{0,2},{1,3},{2,0},{3,1},{4,6},{5,7},{6,4},{7,5},{8,10},{9,11},{10,... | collective-permute-start | bytes 49160 | tf_op jit(solution)/shard_map/ppermute | solution.py:72
  174.4 7.5 %collective-permute-start.14 = (bf16[1,2,32,128]{2,3,1,0:T(8,128)(2,1)S(1)}, bf16[1,2,32,128]{2,3,1,0:T(8,128)(2,1)S(1)}, u32[]{:S(2)}, u32[]{:S(2)}) collective-permute-start(bf16[1,2,32,128]{2,3,1,0:T(8,128)(2,1)S(1)} %get-tuple-element.35), channel_id=1, source_target_pairs={{0,1},{1,0},{2,3},{3,2},{4,5},{5,4},{6,7},{7,6},{8,9},{9,8},{10,11... | collective-permute-start | bytes 49160 | tf_op jit(solution)/shard_map/ppermute | solution.py:72
  175.7 12.7 %collective-permute-start.18 = (bf16[1,2,32,128]{2,3,1,0:T(8,128)(2,1)S(1)}, bf16[1,2,32,128]{2,3,1,0:T(8,128)(2,1)S(1)}, u32[]{:S(2)}, u32[]{:S(2)}) collective-permute-start(bf16[1,2,32,128]{2,3,1,0:T(8,128)(2,1)S(1)} %get-tuple-element.31), channel_id=1, source_target_pairs={{0,5},{1,4},{2,7},{3,6},{4,1},{5,0},{6,3},{7,2},{8,13},{9,12},{10,... | collective-permute-start | bytes 49160 | tf_op jit(solution)/shard_map/ppermute | solution.py:72
  177.0 10.4 %collective-permute-start.16 = (bf16[1,2,32,128]{2,3,1,0:T(8,128)(2,1)S(1)}, bf16[1,2,32,128]{2,3,1,0:T(8,128)(2,1)S(1)}, u32[]{:S(2)}, u32[]{:S(2)}) collective-permute-start(bf16[1,2,32,128]{2,3,1,0:T(8,128)(2,1)S(1)} %get-tuple-element.33), channel_id=1, source_target_pairs={{0,3},{1,2},{2,1},{3,0},{4,7},{5,6},{6,5},{7,4},{8,11},{9,10},{10,... | collective-permute-start | bytes 49160 | tf_op jit(solution)/shard_map/ppermute | solution.py:72
  177.9 10.2 %collective-permute-start.17 = (bf16[1,2,32,128]{2,3,1,0:T(8,128)(2,1)S(1)}, bf16[1,2,32,128]{2,3,1,0:T(8,128)(2,1)S(1)}, u32[]{:S(2)}, u32[]{:S(2)}) collective-permute-start(bf16[1,2,32,128]{2,3,1,0:T(8,128)(2,1)S(1)} %get-tuple-element.32), channel_id=1, source_target_pairs={{0,4},{1,5},{2,6},{3,7},{4,0},{5,1},{6,2},{7,3},{8,12},{9,13},{10,... | collective-permute-start | bytes 49160 | tf_op jit(solution)/shard_map/ppermute | solution.py:72
  180.5 8.6 %collective-permute-start.19 = (bf16[1,2,32,128]{2,3,1,0:T(8,128)(2,1)S(1)}, bf16[1,2,32,128]{2,3,1,0:T(8,128)(2,1)S(1)}, u32[]{:S(2)}, u32[]{:S(2)}) collective-permute-start(bf16[1,2,32,128]{2,3,1,0:T(8,128)(2,1)S(1)} %get-tuple-element.30), channel_id=1, source_target_pairs={{0,6},{1,7},{2,4},{3,5},{4,2},{5,3},{6,0},{7,1},{8,14},{9,15},{10,... | collective-permute-start | bytes 49160 | tf_op jit(solution)/shard_map/ppermute | solution.py:72
  181.9 7.9 %collective-permute-start.20 = (bf16[1,2,32,128]{2,3,1,0:T(8,128)(2,1)S(1)}, bf16[1,2,32,128]{2,3,1,0:T(8,128)(2,1)S(1)}, u32[]{:S(2)}, u32[]{:S(2)}) collective-permute-start(bf16[1,2,32,128]{2,3,1,0:T(8,128)(2,1)S(1)} %get-tuple-element.29), channel_id=1, source_target_pairs={{0,7},{1,6},{2,5},{3,4},{4,3},{5,2},{6,1},{7,0},{8,15},{9,14},{10,... | collective-permute-start | bytes 49160 | tf_op jit(solution)/shard_map/ppermute | solution.py:72
  (10 other events, 11.6 us)
